TPU v7x, 32 devices: a whole 2x2x4 slice. The times are simulated.
32 devices in a mesh: rep: 4 (over y, x), shard: 8 (over z, core).
Axes of the slice: x: 2, y: 2, z: 4, core: 2. Of those that a mesh axis runs over, the one named last changes fastest.
Arguments:
- inputs: bfloat16 [4, 1792, 768], P('rep', 'shard'), may hold values from -6 to 6
- cotangent: bfloat16 [4, 1792, 768], P('rep', 'shard'), may hold values from -6 to 6
- lengths: int32 [4], P('rep'), may hold values from 448 to 1792, as said below
- w_query: bfloat16 [768, 768], P('shard'), may hold values from -0.3125 to 0.3125
- w_key: bfloat16 [768, 768], P('shard'), may hold values from -0.3125 to 0.3125
- w_value: bfloat16 [768, 768], P('shard'), may hold values from -0.21875 to 0.21875
- w_out: bfloat16 [768, 768], P('shard'), may hold values from -1.25 to 1.25
- b_query: bfloat16 [768], P('shard'), may hold values from -1.5 to 1.5
- b_value: bfloat16 [768], P('shard'), may hold values from -0.25 to 0.25
- b_out: bfloat16 [768], P('shard'), may hold values from -1.5 to 1.5
- gain_one: bfloat16 [768], P('shard'), may hold values from 0.5 to 1.5
- shift_one: bfloat16 [768], P('shard'), may hold values from -1.5 to 1.5
- w_up: bfloat16 [768, 3072], P('shard'), may hold values from -0.21875 to 0.21875
- b_up: bfloat16 [3072], P('shard'), may hold values from -1.5 to 1.5
- w_down: bfloat16 [3072, 768], P('shard'), may hold values from -0.15625 to 0.15625
- b_down: bfloat16 [768], P('shard'), may hold values from -1.5 to 1.5
- gain_two: bfloat16 [768], P('shard'), may hold values from 0.5 to 1.5
- shift_two: bfloat16 [768], P('shard'), may hold values from -1.5 to 1.5
Outputs:
- layer_output: bfloat16 [4, 1792, 768], P('rep', 'shard')
- input_grad: float32 [4, 1792, 768], P('rep', 'shard')
- grad_w_query: float32 [768, 768], P('shard')
- grad_w_key: float32 [768, 768], P('shard')
- grad_w_value: float32 [768, 768], P('shard')
- grad_w_out: float32 [768, 768], P('shard')
- grad_b_query: float32 [768], P('shard')
- grad_b_value: float32 [768], P('shard')
- grad_b_out: float32 [768], P('shard')
- grad_gain_one: float32 [768], P('shard')
- grad_shift_one: float32 [768], P('shard')
- grad_w_up: float32 [768, 3072], P('shard')
- grad_b_up: float32 [3072], P('shard')
- grad_w_down: float32 [3072, 768], P('shard')
- grad_b_down: float32 [768], P('shard')
- grad_gain_two: float32 [768], P('shard')
- grad_shift_two: float32 [768], P('shard')
Inputs may be any that keep to these rules, and one draw needn't show every extreme that they name: `lengths`: slot 0 is full; the others hold between a quarter of 1792 and 1792 valid tokens.
All inputs are finite; a program needn't handle non-finite values.
Results may differ from a plain program's by a relative error of at most 0.024.
Values may be sent and summed in bfloat16 or wider, within the bound.
No kernel may reach another device: no remote copies, remote signals or barrier semaphores. Data moves between devices by JAX's collectives and lax.ppermute only.
A program may use at most 256 MiB of HBM per device.

v0:
```python
import math

import jax
import jax.numpy as jnp
from jax import lax
from jax.sharding import PartitionSpec as P

HEADS = 12
HEAD_DIM = 64


epsilon = 1e-05
floor_value = -1e30


def inner_rows(left, right):
    return lax.dot_general(
        left, right, (((0,), (0,)), ((), ())), preferred_element_type=jnp.float32
    )


def times_transposed(left, right):
    return lax.dot_general(
        left, right, (((1,), (1,)), ((), ())), preferred_element_type=jnp.float32
    )


def plain_product(left, right):
    return jnp.dot(left, right, preferred_element_type=jnp.float32)


def norm_forward(hidden, gain, shift):
    center = hidden - jnp.mean(hidden, axis=1, keepdims=True)
    inverse = lax.rsqrt(jnp.mean(center * center, axis=1, keepdims=True) + epsilon)
    scaled = center * inverse
    return (scaled * gain.astype(jnp.float32) + shift.astype(jnp.float32), scaled, inverse)


def norm_backward(grad_out, gain, scaled, inverse):
    grad_scaled = grad_out * gain.astype(jnp.float32)
    grad_in = inverse * (
        grad_scaled
        - jnp.mean(grad_scaled, axis=1, keepdims=True)
        - scaled * jnp.mean(grad_scaled * scaled, axis=1, keepdims=True)
    )
    return (grad_in, jnp.sum(grad_out * scaled, axis=0), jnp.sum(grad_out, axis=0))


def gelu_both(upward):
    cumulative = 0.5 * (1.0 + lax.erf(upward * 0.7071067811865476))
    density = jnp.exp(-0.5 * upward * upward) * 0.3989422804014327
    return (upward * cumulative, cumulative + upward * density)


def split_heads(rows):
    return rows.reshape(rows.shape[0], HEADS, HEAD_DIM)


def column_sum(values_low):
    return jnp.sum(values_low.astype(jnp.float32), axis=0)


def body(
    inputs,
    cotangent,
    lengths,
    w_query,
    w_key,
    w_value,
    w_out,
    b_query,
    b_value,
    b_out,
    gain_one,
    shift_one,
    w_up,
    b_up,
    w_down,
    b_down,
    gain_two,
    shift_two,
):
    gathered = (
        lax.all_gather(w_query, "shard", axis=0, tiled=True),
        lax.all_gather(w_key, "shard", axis=0, tiled=True),
        lax.all_gather(w_value, "shard", axis=0, tiled=True),
        lax.all_gather(w_out, "shard", axis=0, tiled=True),
        lax.all_gather(b_query, "shard", axis=0, tiled=True),
        lax.all_gather(b_value, "shard", axis=0, tiled=True),
        lax.all_gather(b_out, "shard", axis=0, tiled=True),
        lax.all_gather(gain_one, "shard", axis=0, tiled=True),
        lax.all_gather(shift_one, "shard", axis=0, tiled=True),
        lax.all_gather(w_up, "shard", axis=0, tiled=True),
        lax.all_gather(b_up, "shard", axis=0, tiled=True),
        lax.all_gather(w_down, "shard", axis=0, tiled=True),
        lax.all_gather(b_down, "shard", axis=0, tiled=True),
        lax.all_gather(gain_two, "shard", axis=0, tiled=True),
        lax.all_gather(shift_two, "shard", axis=0, tiled=True),
    )
    (
        query_full,
        key_full,
        value_full,
        out_full,
        bias_query,
        bias_value,
        bias_out,
        gain_first,
        shift_first,
        up_full,
        bias_up,
        down_full,
        bias_down,
        gain_second,
        shift_second,
    ) = gathered
    tokens = inputs[0]
    rows = tokens.shape[0]
    model = tokens.shape[1]
    scale = HEAD_DIM ** (-0.5)
    length = lengths[0]
    positions = lax.axis_index("shard") * rows + jnp.arange(rows, dtype=jnp.int32)
    own_valid = positions < length
    row_valid = own_valid.astype(jnp.float32)
    source = tokens.astype(jnp.float32)
    query = (plain_product(tokens, query_full) + bias_query.astype(jnp.float32)).astype(
        jnp.bfloat16
    )
    keys = plain_product(tokens, key_full).astype(jnp.bfloat16)
    values = (plain_product(tokens, value_full) + bias_value.astype(jnp.float32)).astype(
        jnp.bfloat16
    )
    pairs = lax.all_gather(jnp.concatenate([keys, values], axis=1), "shard", axis=0, tiled=True)
    total = pairs.shape[0]
    block = math.gcd(total, 1024)
    count = total // block
    query_heads = split_heads(query)

    def block_scores(index):
        start = index * block
        piece = lax.dynamic_slice_in_dim(pairs, start, block, 0)
        key_heads = split_heads(piece[:, :model])
        value_heads = split_heads(piece[:, model:])
        scores = (
            jnp.einsum("qhd,khd->hqk", query_heads, key_heads, preferred_element_type=jnp.float32)
            * scale
        )
        key_valid = start + jnp.arange(block, dtype=jnp.int32) < length
        return (scores, key_valid[None, None, :], key_heads, value_heads)

    def running_max(index, carry):
        highest, summed = carry
        scores, key_valid, key_heads, value_heads = block_scores(index)
        masked = jnp.where(key_valid, scores, floor_value)
        newest = jnp.maximum(highest, jnp.max(masked, axis=2))
        weights = jnp.where(key_valid, jnp.exp(masked - newest[:, :, None]), 0.0)
        return (newest, summed * jnp.exp(highest - newest) + jnp.sum(weights, axis=2))

    start_max = jnp.full((HEADS, rows), floor_value, jnp.float32)
    highest, summed = lax.fori_loop(
        0, count, running_max, (start_max, jnp.zeros((HEADS, rows), jnp.float32))
    )
    log_total = highest + jnp.log(summed)

    def weighted(index, mixed_sum):
        scores, key_valid, key_heads, value_heads = block_scores(index)
        probs = jnp.where(key_valid, jnp.exp(scores - log_total[:, :, None]), 0.0).astype(
            jnp.bfloat16
        )
        return mixed_sum + jnp.einsum(
            "hqk,khd->qhd", probs, value_heads, preferred_element_type=jnp.float32
        )

    mixed = lax.fori_loop(0, count, weighted, jnp.zeros((rows, HEADS, HEAD_DIM), jnp.float32))
    mixed_low = mixed.reshape(rows, model).astype(jnp.bfloat16)
    branch = plain_product(mixed_low, out_full) + bias_out.astype(jnp.float32)
    normed, scaled_one, inverse_one = norm_forward(source + branch, gain_first, shift_first)
    normed_low = normed.astype(jnp.bfloat16)
    upward = plain_product(normed_low, up_full) + bias_up.astype(jnp.float32)
    active, slope = gelu_both(upward)
    active_low = active.astype(jnp.bfloat16)
    second = plain_product(active_low, down_full) + bias_down.astype(jnp.float32)
    result, scaled_two, inverse_two = norm_forward(normed + second, gain_second, shift_second)
    backward_params = (
        lax.all_gather(w_query, "shard", axis=0, tiled=True),
        lax.all_gather(w_key, "shard", axis=0, tiled=True),
        lax.all_gather(w_value, "shard", axis=0, tiled=True),
        lax.all_gather(w_out, "shard", axis=0, tiled=True),
        lax.all_gather(b_query, "shard", axis=0, tiled=True),
        lax.all_gather(b_value, "shard", axis=0, tiled=True),
        lax.all_gather(b_out, "shard", axis=0, tiled=True),
        lax.all_gather(gain_one, "shard", axis=0, tiled=True),
        lax.all_gather(shift_one, "shard", axis=0, tiled=True),
        lax.all_gather(w_up, "shard", axis=0, tiled=True),
        lax.all_gather(b_up, "shard", axis=0, tiled=True),
        lax.all_gather(w_down, "shard", axis=0, tiled=True),
        lax.all_gather(b_down, "shard", axis=0, tiled=True),
        lax.all_gather(gain_two, "shard", axis=0, tiled=True),
        lax.all_gather(shift_two, "shard", axis=0, tiled=True),
    )
    query_back = backward_params[0]
    key_back = backward_params[1]
    value_back = backward_params[2]
    out_back = backward_params[3]
    gain_first_back = backward_params[7]
    up_back = backward_params[9]
    down_back = backward_params[11]
    gain_second_back = backward_params[13]
    grad_result = cotangent[0].astype(jnp.float32) * row_valid[:, None]
    grad_sum_two, grad_gain_second, grad_shift_second = norm_backward(
        grad_result, gain_second_back, scaled_two, inverse_two
    )
    grad_second = grad_sum_two.astype(jnp.bfloat16)
    grad_down = inner_rows(active_low, grad_second)
    grad_bias_down = column_sum(grad_second)
    grad_upward = (times_transposed(grad_second, down_back) * slope).astype(jnp.bfloat16)
    grad_up = inner_rows(normed_low, grad_upward)
    grad_bias_up = column_sum(grad_upward)
    grad_normed = grad_sum_two + times_transposed(grad_upward, up_back)
    grad_sum_one, grad_gain_first, grad_shift_first = norm_backward(
        grad_normed, gain_first_back, scaled_one, inverse_one
    )
    grad_branch = grad_sum_one.astype(jnp.bfloat16)
    grad_out_proj = inner_rows(mixed_low, grad_branch)
    grad_bias_out = column_sum(grad_branch)
    grad_mixed = times_transposed(grad_branch, out_back).astype(jnp.bfloat16)
    grad_mixed_heads = split_heads(grad_mixed)
    delta = jnp.einsum("qhd,qhd->hq", grad_mixed_heads.astype(jnp.float32), mixed)

    def key_grads(index, carry):
        grad_query_sum, buffer = carry
        scores, key_valid, key_heads, value_heads = block_scores(index)
        probs = jnp.where(key_valid, jnp.exp(scores - log_total[:, :, None]), 0.0)
        probs_low = probs.astype(jnp.bfloat16)
        grad_probs = jnp.einsum(
            "qhd,khd->hqk", grad_mixed_heads, value_heads, preferred_element_type=jnp.float32
        )
        grad_scores = (probs * (grad_probs - delta[:, :, None])).astype(jnp.bfloat16)
        grad_query_sum = (
            grad_query_sum
            + jnp.einsum("hqk,khd->qhd", grad_scores, key_heads, preferred_element_type=jnp.float32)
            * scale
        )
        key_part = (
            jnp.einsum("hqk,qhd->khd", grad_scores, query_heads, preferred_element_type=jnp.float32)
            * scale
        )
        value_part = jnp.einsum(
            "hqk,qhd->khd", probs_low, grad_mixed_heads, preferred_element_type=jnp.float32
        )
        update = jnp.concatenate(
            [key_part.reshape(block, model), value_part.reshape(block, model)], axis=1
        )
        buffer = lax.dynamic_update_slice_in_dim(buffer, update, index * block, 0)
        return (grad_query_sum, buffer)

    grad_query_sum, buffer = lax.fori_loop(
        0,
        count,
        key_grads,
        (
            jnp.zeros((rows, HEADS, HEAD_DIM), jnp.float32),
            jnp.zeros((total, 2 * model), jnp.float32),
        ),
    )
    grad_pairs = lax.psum_scatter(
        buffer.astype(jnp.bfloat16), "shard", scatter_dimension=0, tiled=True
    ).astype(jnp.float32)
    grad_query = grad_query_sum.reshape(rows, model)
    grad_keys = grad_pairs[:, :model]
    grad_values = grad_pairs[:, model:]
    query_low = grad_query.astype(jnp.bfloat16)
    keys_low = grad_keys.astype(jnp.bfloat16)
    values_low = grad_values.astype(jnp.bfloat16)
    grad_query_proj = inner_rows(tokens, query_low)
    grad_key_proj = inner_rows(tokens, keys_low)
    grad_value_proj = inner_rows(tokens, values_low)
    grad_bias_query = column_sum(query_low)
    grad_bias_value = column_sum(values_low)
    grad_input = (
        grad_sum_one
        + times_transposed(query_low, query_back)
        + times_transposed(keys_low, key_back)
        + times_transposed(values_low, value_back)
    )
    shared = (
        lax.psum_scatter(
            grad_query_proj.astype(jnp.bfloat16), "shard", scatter_dimension=0, tiled=True
        ).astype(jnp.float32),
        lax.psum_scatter(
            grad_key_proj.astype(jnp.bfloat16), "shard", scatter_dimension=0, tiled=True
        ).astype(jnp.float32),
        lax.psum_scatter(
            grad_value_proj.astype(jnp.bfloat16), "shard", scatter_dimension=0, tiled=True
        ).astype(jnp.float32),
        lax.psum_scatter(
            grad_out_proj.astype(jnp.bfloat16), "shard", scatter_dimension=0, tiled=True
        ).astype(jnp.float32),
        lax.psum_scatter(
            grad_bias_query.astype(jnp.bfloat16), "shard", scatter_dimension=0, tiled=True
        ).astype(jnp.float32),
        lax.psum_scatter(
            grad_bias_value.astype(jnp.bfloat16), "shard", scatter_dimension=0, tiled=True
        ).astype(jnp.float32),
        lax.psum_scatter(
            grad_bias_out.astype(jnp.bfloat16), "shard", scatter_dimension=0, tiled=True
        ).astype(jnp.float32),
        lax.psum_scatter(
            grad_gain_first.astype(jnp.bfloat16), "shard", scatter_dimension=0, tiled=True
        ).astype(jnp.float32),
        lax.psum_scatter(
            grad_shift_first.astype(jnp.bfloat16), "shard", scatter_dimension=0, tiled=True
        ).astype(jnp.float32),
        lax.psum_scatter(
            grad_up.astype(jnp.bfloat16), "shard", scatter_dimension=0, tiled=True
        ).astype(jnp.float32),
        lax.psum_scatter(
            grad_bias_up.astype(jnp.bfloat16), "shard", scatter_dimension=0, tiled=True
        ).astype(jnp.float32),
        lax.psum_scatter(
            grad_down.astype(jnp.bfloat16), "shard", scatter_dimension=0, tiled=True
        ).astype(jnp.float32),
        lax.psum_scatter(
            grad_bias_down.astype(jnp.bfloat16), "shard", scatter_dimension=0, tiled=True
        ).astype(jnp.float32),
        lax.psum_scatter(
            grad_gain_second.astype(jnp.bfloat16), "shard", scatter_dimension=0, tiled=True
        ).astype(jnp.float32),
        lax.psum_scatter(
            grad_shift_second.astype(jnp.bfloat16), "shard", scatter_dimension=0, tiled=True
        ).astype(jnp.float32),
    )
    (
        part_query,
        part_key,
        part_value,
        part_out,
        part_bias_query,
        part_bias_value,
        part_bias_out,
        part_gain_first,
        part_shift_first,
        part_up,
        part_bias_up,
        part_down,
        part_bias_down,
        part_gain_second,
        part_shift_second,
    ) = shared
    summed = (
        lax.psum(part_query.astype(jnp.bfloat16), "rep").astype(jnp.float32),
        lax.psum(part_key.astype(jnp.bfloat16), "rep").astype(jnp.float32),
        lax.psum(part_value.astype(jnp.bfloat16), "rep").astype(jnp.float32),
        lax.psum(part_out.astype(jnp.bfloat16), "rep").astype(jnp.float32),
        lax.psum(part_bias_query.astype(jnp.bfloat16), "rep").astype(jnp.float32),
        lax.psum(part_bias_value.astype(jnp.bfloat16), "rep").astype(jnp.float32),
        lax.psum(part_bias_out.astype(jnp.bfloat16), "rep").astype(jnp.float32),
        lax.psum(part_gain_first.astype(jnp.bfloat16), "rep").astype(jnp.float32),
        lax.psum(part_shift_first.astype(jnp.bfloat16), "rep").astype(jnp.float32),
        lax.psum(part_up.astype(jnp.bfloat16), "rep").astype(jnp.float32),
        lax.psum(part_bias_up.astype(jnp.bfloat16), "rep").astype(jnp.float32),
        lax.psum(part_down.astype(jnp.bfloat16), "rep").astype(jnp.float32),
        lax.psum(part_bias_down.astype(jnp.bfloat16), "rep").astype(jnp.float32),
        lax.psum(part_gain_second.astype(jnp.bfloat16), "rep").astype(jnp.float32),
        lax.psum(part_shift_second.astype(jnp.bfloat16), "rep").astype(jnp.float32),
    )
    return (result.astype(jnp.bfloat16)[None], grad_input[None]) + tuple(summed)


def solution(mesh):
    placed = (
        P("rep", "shard", None),
        P("rep", "shard", None),
        P("rep"),
        P("shard", None),
        P("shard", None),
        P("shard", None),
        P("shard", None),
        P("shard"),
        P("shard"),
        P("shard"),
        P("shard"),
        P("shard"),
        P("shard", None),
        P("shard"),
        P("shard", None),
        P("shard"),
        P("shard"),
        P("shard"),
    )
    return jax.shard_map(
        body,
        mesh=mesh,
        in_specs=placed,
        out_specs=(
            P("rep", "shard", None),
            P("rep", "shard", None),
            P("shard", None),
            P("shard", None),
            P("shard", None),
            P("shard", None),
            P("shard"),
            P("shard"),
            P("shard"),
            P("shard"),
            P("shard"),
            P("shard", None),
            P("shard"),
            P("shard", None),
            P("shard"),
            P("shard"),
            P("shard"),
        ),
        check_vma=False,
    )
```

profile of v0, /device:TPU:0, one launch (start us, length us, event | category | flops | bytes accessed | tf_op | source)
XLA Modules:
  0.0 737.3 jit_solution(4788529265016331617)
XLA Ops:
  17.3 30.8 %all-reduce.18 = (bf16[768]{0:T(1024)(128)(2,1)S(1)}, bf16[768]{0:T(1024)(128)(2,1)S(1)}, bf16[768]{0:T(1024)(128)(2,1)S(1)}, bf16[768]{0:T(1024)(128)(2,1)S(1)}...) all-reduce(bf16[768]{0:T(1024)(128)(2,1)S(1)} %dynamic-update-slice, ...), channel_id=1, replica_groups=mesh['rep'=4,'shard'=8] {'shard'}, use_global_device_ids=true, to_apply=%add | all-reduce | flops 5376 | bytes 21504
  50.0 9.5 %all-gather.11.cloned.1.call-done = bf16[768,768]{1,0:T(8,128)(2,1)} async-done(((bf16[96,768]{1,0:T(8,128)(2,1)}), bf16[768,768]{1,0:T(8,128)(2,1)}) %all-gather.11.cloned.1.call-update) | async-done | bytes 1179664 | tf_op jit(solution)/shard_map/all_gather | solution.py:86
  64.9 13.0 %all-gather = bf16[8,1,384]{2,1,0:T(2,128)(2,1)S(1)} all-gather(bf16[1,1,384]{2,1,0:T(2,128)(2,1)S(1)} %reshape.198), channel_id=1, replica_groups=mesh['rep'=4,'shard'=8] {'shard'}, dimensions={0}, use_global_device_ids=true | all-gather | bytes 6912 | tf_op jit(solution)/shard_map/all_gather | solution.py:94
  78.0 5.5 all-gather.15.cloned.1.call-done
  85.4 58.1 %all-gather.13.cloned.1.call-done = bf16[1792,1536]{1,0:T(8,128)(2,1)} async-done(((bf16[224,1536]{1,0:T(8,128)(2,1)}), bf16[1792,1536]{1,0:T(8,128)(2,1)}) %all-gather.13.cloned.1.call-update) | async-done | bytes 5505040 | tf_op jit(solution)/shard_map/all_gather | solution.py:133
  143.5 8.3 %copy.55 = bf16[1792,1536]{0,1:T(8,128)(2,1)} copy(bf16[1792,1536]{1,0:T(8,128)(2,1)} %all-gather.13.cloned.1.call-done) | data formatting | bytes 11010048
  151.8 25.8 %while.46 = (s32[]{:T(128)}, f32[12,224]{1,0:T(8,128)S(1)}, f32[12,224]{1,0:T(8,128)S(1)}, s32[]{:T(128)}, bf16[1792,1536]{0,1:T(8,128)(2,1)}, /*index=5*/bf16[2...) while((s32[]{:T(128)}, f32[12,224]{1,0:T(8,128)S(1)}, ...), condition=%wide.region_3.4_spmd.clone, body=%wide.region_0.3_spmd.clone.sunk | while | flops 93599368 | bytes 7169458 | solution.py:160
  177.6 34.2 %while.47 = (s32[]{:T(128)}, f32[224,12,64]{0,2,1:T(8,128)}, bf16[1792,1536]{0,1:T(8,128)(2,1)}, s32[]{:T(128)}, bf16[224,12,64]{0,2,1:T(8,128)(2,1)S(1)}, /*ind...) while((s32[]{:T(128)}, f32[224,12,64]{0,2,1:T(8,128)}, ...), condition=%wide.region_5.6_spmd.clone, body=%wide.region_4.5_spmd.clone.sunk | while | flops 179257856 | bytes 4091081 | solution.py:174
  218.9 5.9 multiply_convert_fusion.1
  224.8 45.7 %all-gather.21.cloned.1.call-done = bf16[3072,768]{1,0:T(8,128)(2,1)} async-done(((bf16[384,768]{1,0:T(8,128)(2,1)}), bf16[3072,768]{1,0:T(8,128)(2,1)}) %all-gather.21.cloned.1.call-update) | async-done | bytes 4718608 | tf_op jit(solution)/shard_map/all_gather | solution.py:95
  290.3 44.6 %while.48 = (s32[]{:T(128)}, f32[224,12,64]{0,2,1:T(8,128)S(1)}, bf16[1792,1536]{0,1:T(8,128)(2,1)}, bf16[1792,1536]{0,1:T(8,128)(2,1)}, s32[]{:T(128)}, /*index...) while((s32[]{:T(128)}, f32[224,12,64]{0,2,1:T(8,128)S(1)}, ...), condition=%wide.region_15.16_spmd.clone, body=%wide.region_14.15_spmd.clone.sunk | while | flops 449765888 | bytes 21660160 | solution.py:257
  334.8 8.3 %copy.69 = bf16[1792,1536]{1,0:T(8,128)(2,1)} copy(bf16[1792,1536]{0,1:T(8,128)(2,1)} %get-tuple-element.395) | data formatting | bytes 11010048
  348.1 56.3 %reduce-scatter.22.cloned.1.call-done = bf16[224,1536]{1,0:T(8,128)(2,1)} async-done(((bf16[1792,1536]{1,0:T(8,128)(2,1)}), bf16[224,1536]{1,0:T(8,128)(2,1)}) %reduce-scatter.22.cloned.1.call-update) | async-done | bytes 688144
  416.0 5.0 convolution_convert_fusion.1
  422.4 4.7 convolution_convert_fusion
  427.2 11.5 %reduce-scatter.24.cloned.1.call-done = bf16[96,768]{1,0:T(8,128)(2,1)} async-done(((bf16[768,768]{1,0:T(8,128)(2,1)}), bf16[96,768]{1,0:T(8,128)(2,1)}) %reduce-scatter.24.cloned.1.call-update) | async-done | bytes 147472
  440.4 31.5 %reduce-scatter.28.cloned.1.call-done = bf16[96,768]{1,0:T(8,128)(2,1)} async-done(((bf16[768,768]{1,0:T(8,128)(2,1)}), bf16[96,768]{1,0:T(8,128)(2,1)}) %reduce-scatter.28.cloned.1.call-update) | async-done | bytes 147472
  473.7 31.9 %reduce-scatter.26.cloned.1.call-done = bf16[96,768]{1,0:T(8,128)(2,1)} async-done(((bf16[768,768]{1,0:T(8,128)(2,1)}), bf16[96,768]{1,0:T(8,128)(2,1)}) %reduce-scatter.26.cloned.1.call-update) | async-done | bytes 147472
  507.3 32.0 %reduce-scatter.16.cloned.1.call-done = bf16[96,768]{1,0:T(8,128)(2,1)} async-done(((bf16[768,768]{1,0:T(8,128)(2,1)}), bf16[96,768]{1,0:T(8,128)(2,1)}) %reduce-scatter.16.cloned.1.call-update) | async-done | bytes 147472 | tf_op jit(solution)/shard_map/reduce_scatter | solution.py:296
  539.3 55.5 %reduce-scatter.18.cloned.1.call-done = bf16[96,3072]{1,0:T(8,128)(2,1)} async-done(((bf16[768,3072]{1,0:T(8,128)(2,1)}), bf16[96,3072]{1,0:T(8,128)(2,1)}) %reduce-scatter.18.cloned.1.call-update) | async-done | bytes 589840 | tf_op jit(solution)/shard_map/reduce_scatter | solution.py:314
  594.8 55.5 %reduce-scatter.20.cloned.1.call-done = bf16[384,768]{1,0:T(8,128)(2,1)} async-done(((bf16[3072,768]{1,0:T(8,128)(2,1)}), bf16[384,768]{1,0:T(8,128)(2,1)}) %reduce-scatter.20.cloned.1.call-update) | async-done | bytes 589840 | tf_op jit(solution)/shard_map/reduce_scatter | solution.py:320
  654.9 26.0 %all-reduce.17 = (bf16[768]{0:T(1024)(128)(2,1)S(1)}, bf16[768]{0:T(1024)(128)(2,1)S(1)}, bf16[768]{0:T(1024)(128)(2,1)S(1)}, bf16[768]{0:T(1024)(128)(2,1)S(1)}...) all-reduce(bf16[768]{0:T(1024)(128)(2,1)S(1)} %dynamic-update-slice, ...), channel_id=1, replica_groups=mesh['rep'=4,'shard'=8] {'shard'}, use_global_device_ids=true, to_apply=%add.7 | all-reduce | flops 9984 | bytes 39936
  681.6 10.0 %all-reduce.19 = (bf16[96]{0:T(256)(128)(2,1)S(1)}, bf16[96]{0:T(256)(128)(2,1)S(1)}, bf16[96]{0:T(256)(128)(2,1)S(1)}, bf16[96]{0:T(256)(128)(2,1)S(1)}, bf16[9...) all-reduce(bf16[96]{0:T(256)(128)(2,1)S(1)} %dynamic-slice.9, ...), channel_id=1, replica_groups=mesh['rep'=4,'shard'=8] {'rep'}, use_global_device_ids=true, to_apply=%region_27.28 | all-reduce | flops 1152 | bytes 4608 | tf_op jit(solution)/shard_map/psum | solution.py:355
  700.3 20.3 %all-reduce.23.cloned.1.call-done = (bf16[96,768]{0,1:T(8,128)(2,1)}, bf16[96,768]{0,1:T(8,128)(2,1)}, bf16[96,768]{0,1:T(8,128)(2,1)}, bf16[96,768]{1,0:T(8,128...) async-done(((bf16[96,768]{0,1:T(8,128)(2,1)}, bf16[96,768]{0,1:T(8,128)(2,1)}, bf16[96,768]{0,1:T(8,128)(2,1)}, bf16[96,768]{1,0:T(8,128)(2,1)}, ...) | async-done | bytes 1769488 | tf_op jit(solution)/shard_map/psum | solution.py:351
  (329 shorter events, 194.0 us)
Async XLA Ops:
  7.2 40.9 %all-gather.9.cloned.1.call-start = ((), (), s32[]{:S(2)}) async-start(), calls=%async_computation.7 | async-start | bytes 1327104 | tf_op jit(solution)/shard_map/all_gather | solution.py:85
  7.9 51.5 %all-gather.11.cloned.1.call-start = ((), (), s32[]{:S(2)}) async-start(), calls=%async_computation.8 | async-start | bytes 1327104 | tf_op jit(solution)/shard_map/all_gather | solution.py:86
  8.7 74.8 %all-gather.15.cloned.1.call-start = ((), (), s32[]{:S(2)}) async-start(), calls=%async_computation.10 | async-start | bytes 1327104 | tf_op jit(solution)/shard_map/all_gather | solution.py:84
  9.4 134.1 %all-gather.13.cloned.1.call-start = ((), (), s32[]{:S(2)}) async-start(), calls=%async_computation.9 | async-start | bytes 6193152 | tf_op jit(solution)/shard_map/all_gather | solution.py:133
  62.2 150.9 %all-gather.17.cloned.1.call-start = ((), (), s32[]{:S(2)}) async-start(), calls=%async_computation.11 | async-start | bytes 1327104 | tf_op jit(solution)/shard_map/all_gather | solution.py:87
  62.8 156.2 %all-gather.19.cloned.1.call-start = ((), (), s32[]{:S(2)}) async-start(), calls=%async_computation.12 | async-start | bytes 5308416 | tf_op jit(solution)/shard_map/all_gather | solution.py:93
  63.4 207.2 %all-gather.21.cloned.1.call-start = ((), (), s32[]{:S(2)}) async-start(), calls=%async_computation.13 | async-start | bytes 5308416 | tf_op jit(solution)/shard_map/all_gather | solution.py:95
  64.1 340.3 %reduce-scatter.22.cloned.1.call-start = ((), (), s32[]{:S(2)}) async-start(), calls=%async_computation.17 | async-start | bytes 6193152
  343.2 95.5 %reduce-scatter.24.cloned.1.call-start = ((), (), s32[]{:S(2)}) async-start(), calls=%async_computation.18 | async-start | bytes 1327104
  348.0 123.9 %reduce-scatter.28.cloned.1.call-start = ((), (), s32[]{:S(2)}) async-start(), calls=%async_computation.20 | async-start | bytes 1327104
  409.4 96.2 %reduce-scatter.26.cloned.1.call-start = ((), (), s32[]{:S(2)}) async-start(), calls=%async_computation.19 | async-start | bytes 1327104
  413.4 125.9 %reduce-scatter.16.cloned.1.call-start = ((), (), s32[]{:S(2)}) async-start(), calls=%async_computation.14 | async-start | bytes 1327104 | tf_op jit(solution)/shard_map/reduce_scatter | solution.py:296
  415.9 178.8 %reduce-scatter.18.cloned.1.call-start = ((), (), s32[]{:S(2)}) async-start(), calls=%async_computation.15 | async-start | bytes 5308416 | tf_op jit(solution)/shard_map/reduce_scatter | solution.py:314
  421.1 229.2 %reduce-scatter.20.cloned.1.call-start = ((), (), s32[]{:S(2)}) async-start(), calls=%async_computation.16 | async-start | bytes 5308416 | tf_op jit(solution)/shard_map/reduce_scatter | solution.py:320
  427.1 224.5 %copy-start.22 = (bf16[96]{0:T(256)(128)(2,1)S(1)}, bf16[96]{0:T(256)(128)(2,1)}, u32[]{:S(2)}) copy-start(bf16[96]{0:T(256)(128)(2,1)} %param.41) | copy-start | bytes 580
  427.1 293.4 %all-reduce.23.cloned.1.call-start = ((), (), s32[]{:S(2)}) async-start(), calls=%async_computation.21 | async-start | bytes 3833856 | tf_op jit(solution)/shard_map/psum | solution.py:351
  473.6 181.2 %copy-start.14 = (bf16[768]{0:T(1024)(128)(2,1)S(1)}, bf16[768]{0:T(1024)(128)(2,1)}, u32[]{:S(2)}) copy-start(bf16[768]{0:T(1024)(128)(2,1)} %get-tuple-element.584) | copy-start | bytes 4612
  473.6 181.2 %copy-start.15 = (bf16[768]{0:T(1024)(128)(2,1)S(1)}, bf16[768]{0:T(1024)(128)(2,1)}, u32[]{:S(2)}) copy-start(bf16[768]{0:T(1024)(128)(2,1)} %get-tuple-element.589) | copy-start | bytes 4612
  473.6 181.2 %copy-start.16 = (bf16[768]{0:T(1024)(128)(2,1)S(1)}, bf16[768]{0:T(1024)(128)(2,1)}, u32[]{:S(2)}) copy-start(bf16[768]{0:T(1024)(128)(2,1)} %get-tuple-element.664) | copy-start | bytes 4612
  473.6 181.2 %copy-start.17 = (bf16[768]{0:T(1024)(128)(2,1)S(1)}, bf16[768]{0:T(1024)(128)(2,1)}, u32[]{:S(2)}) copy-start(bf16[768]{0:T(1024)(128)(2,1)} %get-tuple-element.666) | copy-start | bytes 4612
  473.6 181.2 %copy-start.18 = (bf16[3072]{0:T(1024)(128)(2,1)S(1)}, bf16[3072]{0:T(1024)(128)(2,1)}, u32[]{:S(2)}) copy-start(bf16[3072]{0:T(1024)(128)(2,1)} %get-tuple-element.685) | copy-start | bytes 18436
  473.7 181.2 %copy-start.19 = (bf16[768]{0:T(1024)(128)(2,1)S(1)}, bf16[768]{0:T(1024)(128)(2,1)}, u32[]{:S(2)}) copy-start(bf16[768]{0:T(1024)(128)(2,1)} %get-tuple-element.582) | copy-start | bytes 4612
  473.7 181.2 %copy-start.20 = (bf16[768]{0:T(1024)(128)(2,1)S(1)}, bf16[768]{0:T(1024)(128)(2,1)}, u32[]{:S(2)}) copy-start(bf16[768]{0:T(1024)(128)(2,1)} %get-tuple-element.587) | copy-start | bytes 4612
  507.3 189.1 %copy-start.2 = (bf16[768,768]{1,0:T(8,128)(2,1)S(1)}, bf16[768,768]{1,0:T(8,128)(2,1)}, u32[]{:S(2)}) copy-start(bf16[768,768]{1,0:T(8,128)(2,1)} %all-gather.9.cloned.1.call-done) | copy-start | bytes 3538948
  (25 other events, 135.2 us)
Sparse Core Ops, SparseCore 0:
  9.6 25.6 all-gather.8
  36.9 22.4 all-gather.10
  61.1 22.3 all-gather.14
  85.6 57.9 all-gather.12
  145.0 21.5 all-gather.16
  168.1 50.8 all-gather.18
  220.6 49.9 all-gather.20
  343.3 61.0 reduce-scatter.21
  407.2 31.3 reduce-scatter.23
  440.8 31.0 reduce-scatter.27
  474.2 31.2 reduce-scatter.25
  508.2 30.9 reduce-scatter.15
  541.6 53.1 reduce-scatter.17
  596.9 53.3 reduce-scatter.19
  654.6 65.8 all-reduce.22
where the time goes:
time: 740 us; the launch traced here: 737 us
  waiting for transfers between devices  421 us (57%)
  matrix products  97.8 us (13%)
  blocking collectives  79.9 us (11%)
  local copies, waits for them, and re-layouts  73.4 us (10%)
  other arithmetic  46.8 us (6%)
  between operations  17 us (2%)
    unnamed x19, waiting for transfers between devices  135 us
    all_gather x1, waiting for transfers between devices, body(): lax.all_gather(jnp.concatenate([keys, values], axis=1), 'shard', axis=0,...  58.1 us
    unnamed x2, blocking collectives  56.8 us
    reduce_scatter x1, waiting for transfers between devices, body(): lax.psum_scatter(grad_up.astype(jnp.bfloat16), 'shard', scatter_dimension...  55.5 us
    reduce_scatter x1, waiting for transfers between devices, body(): lax.psum_scatter(grad_down.astype(jnp.bfloat16), 'shard', scatter_dimensi...  55.5 us
    all_gather x1, waiting for transfers between devices, body(): lax.all_gather(w_down, 'shard', axis=0, tiled=True)  45.7 us
    unnamed x92, local copies, waits for them, and re-layouts  44.5 us
    reduce_scatter x1, waiting for transfers between devices, body(): lax.psum_scatter(grad_out_proj.astype(jnp.bfloat16), 'shard', scatter_dim...  32 us
  transfers between devices with their start and end apart: 15, of which 13 were waited for; matrix products, arithmetic and copies ran while one was open for 18% of the time, Pallas kernels for 0%

commit v1 on v0

v1 whole, which is shorter than its diff:
```python
import math

import jax
import jax.numpy as jnp
from jax import lax
from jax.experimental import pallas as pl
from jax.experimental.pallas import tpu as pltpu
from jax.sharding import PartitionSpec as P

HEADS = 12
HEAD_DIM = 64
SCALE = HEAD_DIM ** (-0.5)

epsilon = 1e-05
floor_value = -1e30
f32 = jnp.float32
bf16 = jnp.bfloat16


def dot(left, right, left_dim, right_dim):
    return lax.dot_general(
        left, right, (((left_dim,), (right_dim,)), ((), ())), preferred_element_type=f32
    )


def three_parts(value):
    first = value.astype(bf16)
    rest = value - first.astype(f32)
    second = rest.astype(bf16)
    third = (rest - second.astype(f32)).astype(bf16)
    return first, second, third


def extra_rows(rows, width):
    index = lax.broadcasted_iota(jnp.int32, (HEAD_DIM, width), 0)
    block = jnp.zeros((HEAD_DIM, width), f32)
    for place, row in enumerate(rows):
        block = jnp.where(index == place, row, block)
    return block.astype(bf16)


def forward_kernel(q_ref, kv_ref, aug_ref, o_ref, ot_ref, lse_ref, acc_ref, max_ref, sum_ref, *, block):
    width = q_ref.shape[0]
    heads = width // HEAD_DIM
    keys = kv_ref.shape[1]
    queries = q_ref.shape[1]
    unit = extra_rows([1.0], queries)
    wide = [
        jnp.concatenate([q_ref[h * HEAD_DIM : (h + 1) * HEAD_DIM, :], unit], axis=0)
        for h in range(heads)
    ]
    acc_ref[...] = jnp.zeros(acc_ref.shape, f32)
    sum_ref[...] = jnp.zeros(sum_ref.shape, f32)
    max_ref[...] = jnp.full(max_ref.shape, 2 * floor_value, f32)

    def step(index, carry):
        span = pl.ds(pl.multiple_of(index * block, block), block)
        aug = aug_ref[:, span]
        for h in range(heads):
            part = slice(h * HEAD_DIM, (h + 1) * HEAD_DIM)
            key = jnp.concatenate([kv_ref[part, span], aug], axis=0).T
            scores = dot(key, wide[h], 1, 0)
            old = max_ref[h : h + 1, :]
            newest = jnp.maximum(old, jnp.max(scores, axis=0, keepdims=True))
            alpha = jnp.exp(old - newest)
            weights = jnp.exp(scores - newest)
            max_ref[h : h + 1, :] = newest
            sum_ref[h : h + 1, :] = sum_ref[h : h + 1, :] * alpha + jnp.sum(
                weights, axis=0, keepdims=True
            )
            value = kv_ref[width + h * HEAD_DIM : width + (h + 1) * HEAD_DIM, span]
            acc_ref[part, :] = acc_ref[part, :] * alpha + dot(value, weights.astype(bf16), 1, 0)
        return carry

    lax.fori_loop(0, keys // block, step, 0)
    for h in range(heads):
        part = slice(h * HEAD_DIM, (h + 1) * HEAD_DIM)
        total = sum_ref[h : h + 1, :]
        ot_ref[part, :] = acc_ref[part, :] / total
        lse_ref[h : h + 1, :] = max_ref[h : h + 1, :] + jnp.log(total)
    o_ref[...] = ot_ref[...].astype(bf16).T


def backward_kernel(q_ref, kv_ref, aug_ref, ot_ref, lse_ref, do_ref, dq_ref, dk_ref, dv_ref, acc_ref, *, block):
    width = q_ref.shape[0]
    heads = width // HEAD_DIM
    keys = kv_ref.shape[1]
    queries = q_ref.shape[1]
    out_grad = do_ref[...]
    out_grad_t = out_grad.T
    query = q_ref[...].T
    lane = lax.broadcasted_iota(jnp.int32, query.shape, 1) // HEAD_DIM
    only_q = [jnp.where(lane == h, query, jnp.zeros_like(query)) for h in range(heads)]
    only_do = [jnp.where(lane == h, out_grad, jnp.zeros_like(query)) for h in range(heads)]
    wide_q = []
    wide_do = []
    for h in range(heads):
        part = slice(h * HEAD_DIM, (h + 1) * HEAD_DIM)
        lse = [-piece.astype(f32) for piece in three_parts(lse_ref[h : h + 1, :])]
        wide_q.append(jnp.concatenate([q_ref[part, :], extra_rows([1.0] + lse, queries)], axis=0))
        delta = jnp.sum(out_grad_t[part, :].astype(f32) * ot_ref[part, :], axis=0, keepdims=True)
        pieces = [-piece.astype(f32) for piece in three_parts(delta)]
        wide_do.append(
            jnp.concatenate([out_grad_t[part, :], extra_rows([0.0] + pieces, queries)], axis=0)
        )
    acc_ref[...] = jnp.zeros(acc_ref.shape, f32)

    def step(index, carry):
        span = pl.ds(pl.multiple_of(index * block, block), block)
        aug = aug_ref[:, span]
        grad_key = jnp.zeros((block, width), f32)
        grad_value = jnp.zeros((block, width), f32)
        for h in range(heads):
            part = slice(h * HEAD_DIM, (h + 1) * HEAD_DIM)
            key_t = kv_ref[part, span]
            value_t = kv_ref[width + h * HEAD_DIM : width + (h + 1) * HEAD_DIM, span]
            key = jnp.concatenate([key_t, aug], axis=0).T
            value = jnp.concatenate([value_t, aug], axis=0).T
            probs = jnp.exp(dot(key, wide_q[h], 1, 0))
            centred = dot(value, wide_do[h], 1, 0)
            low = probs.astype(bf16)
            scores = (probs * centred).astype(bf16)
            grad_key += dot(scores, only_q[h], 1, 0)
            grad_value += dot(low, only_do[h], 1, 0)
            acc_ref[part, :] += dot(key_t, scores, 1, 0)
        dk_ref[span, :] = grad_key.astype(bf16)
        dv_ref[span, :] = grad_value.astype(bf16)
        return carry

    lax.fori_loop(0, keys // block, step, 0)
    dq_ref[...] = (acc_ref[...] * SCALE).astype(bf16).T


def attend_forward(query, pairs, aug):
    width, queries = query.shape
    keys = pairs.shape[1]
    block = math.gcd(keys, 256)
    return pl.pallas_call(
        lambda *refs: forward_kernel(*refs, block=block),
        out_shape=(
            jax.ShapeDtypeStruct((queries, width), bf16),
            jax.ShapeDtypeStruct((width, queries), f32),
            jax.ShapeDtypeStruct((8, queries), f32),
        ),
        scratch_shapes=[
            pltpu.VMEM((width, queries), f32),
            pltpu.VMEM((8, queries), f32),
            pltpu.VMEM((8, queries), f32),
        ],
        name="attend_forward",
    )(query, pairs, aug)


def attend_backward(query, pairs, aug, mixed_t, lse, out_grad):
    width, queries = query.shape
    keys = pairs.shape[1]
    block = math.gcd(keys, 256)
    return pl.pallas_call(
        lambda *refs: backward_kernel(*refs, block=block),
        out_shape=(
            jax.ShapeDtypeStruct((queries, width), bf16),
            jax.ShapeDtypeStruct((keys, width), bf16),
            jax.ShapeDtypeStruct((keys, width), bf16),
        ),
        scratch_shapes=[pltpu.VMEM((width, queries), f32)],
        name="attend_backward",
    )(query, pairs, aug, mixed_t, lse, out_grad)


def norm_forward(hidden, gain, shift):
    center = hidden - jnp.mean(hidden, axis=1, keepdims=True)
    inverse = lax.rsqrt(jnp.mean(center * center, axis=1, keepdims=True) + epsilon)
    scaled = center * inverse
    return (scaled * gain.astype(f32) + shift.astype(f32), scaled, inverse)


def norm_backward(grad_out, gain, scaled, inverse):
    grad_scaled = grad_out * gain.astype(f32)
    grad_in = inverse * (
        grad_scaled
        - jnp.mean(grad_scaled, axis=1, keepdims=True)
        - scaled * jnp.mean(grad_scaled * scaled, axis=1, keepdims=True)
    )
    return (grad_in, jnp.sum(grad_out * scaled, axis=0), jnp.sum(grad_out, axis=0))


def gelu_both(upward):
    cumulative = 0.5 * (1.0 + lax.erf(upward * 0.7071067811865476))
    density = jnp.exp(-0.5 * upward * upward) * 0.3989422804014327
    return (upward * cumulative, cumulative + upward * density)


def column_sum(values_low):
    return jnp.sum(values_low.astype(f32), axis=0)


def make_body(reps, shards):
    groups = math.gcd(HEADS, shards)
    peers = shards // groups

    def swap_group(value, e):
        perm = [(s, s ^ (e * peers)) for s in range(shards)]
        return lax.ppermute(value, "shard", perm)

    def swap_peer(value, d):
        perm = [(s, s ^ d) for s in range(shards)]
        return lax.ppermute(value, "shard", perm)

    def across_reps(value):
        return lax.all_to_all(value, "rep", 0, 0, tiled=True)

    def body(
        inputs,
        cotangent,
        lengths,
        w_query,
        w_key,
        w_value,
        w_out,
        b_query,
        b_value,
        b_out,
        gain_one,
        shift_one,
        w_up,
        b_up,
        w_down,
        b_down,
        gain_two,
        shift_two,
    ):
        tokens = inputs[0]
        rows, model = tokens.shape
        width = model // groups
        small_rows = w_query.shape[0]
        hidden_rows = w_down.shape[0]
        length = lengths[0]
        shard = lax.axis_index("shard")
        group = shard // peers
        peer = shard % peers
        own_valid = shard * rows + jnp.arange(rows, dtype=jnp.int32) < length
        row_valid = own_valid.astype(f32)
        source = tokens.astype(f32)

        blocks = [tokens]
        for e in range(1, groups):
            blocks.append(swap_group(tokens, e))
        x = jnp.concatenate(blocks, axis=0)

        packed = jnp.stack([w_query, w_key, w_value])
        packed = packed.reshape(3, small_rows, groups, width).transpose(2, 0, 1, 3)
        zg = [[g * peers + p for g in range(groups)] for p in range(peers)]
        got = lax.all_to_all(packed, "shard", 0, 0, tiled=True, axis_index_groups=zg)
        got = [got] + [swap_peer(got, d) for d in range(1, peers)]
        order = peer ^ jnp.arange(peers)
        bias = jnp.stack([b_query, b_value])
        bias = jnp.stack([bias] + [swap_peer(bias, d) for d in range(1, peers)])[order]
        bias = bias.transpose(1, 0, 2).reshape(2, width)
        w_heads = jnp.stack(got)[order].transpose(2, 1, 0, 3, 4).reshape(3, model, width)

        w_all = lax.all_gather(
            jnp.concatenate(
                [
                    w_out,
                    jnp.concatenate(
                        [
                            b_out,
                            gain_one,
                            shift_one,
                            b_up,
                            b_down,
                            gain_two,
                            shift_two,
                            jnp.zeros((-(6 * small_rows + b_up.shape[0])) % model, bf16),
                        ]
                    ).reshape(-1, model),
                ]
            ),
            "shard",
            axis=0,
        )
        out_full = w_all[:, :small_rows].reshape(model, model)
        flat = w_all[:, small_rows:].reshape(shards, -1)
        bounds = []
        start = 0
        for item in (b_out, gain_one, shift_one, b_up, b_down, gain_two, shift_two):
            bounds.append(flat[:, start : start + item.shape[0]].reshape(-1))
            start += item.shape[0]
        bias_out, gain_first, shift_first, bias_up, bias_down, gain_second, shift_second = bounds
        up_full = lax.all_gather(w_up, "shard", axis=0, tiled=True)
        down_full = lax.all_gather(w_down, "shard", axis=0, tiled=True)

        query_t = ((dot(w_heads[0], x, 0, 1) + bias[0].astype(f32)[:, None]).astype(bf16)) * SCALE
        key_t = dot(w_heads[1], x, 0, 1).astype(bf16)
        value_t = (dot(w_heads[2], x, 0, 1) + bias[1].astype(f32)[:, None]).astype(bf16)
        pair = jnp.concatenate([key_t, value_t], axis=0)
        pairs = jnp.concatenate([pair] + [swap_peer(pair, d) for d in range(1, peers)], axis=1)
        starts = (
            (group ^ jnp.arange(groups))[None, :] * peers + (peer ^ jnp.arange(peers))[:, None]
        ) * rows
        positions = (starts[:, :, None] + jnp.arange(rows)[None, None, :]).reshape(1, -1)
        keys = positions.shape[1]
        aug = jnp.concatenate(
            [
                jnp.where(positions < length, 0.0, floor_value).astype(bf16),
                jnp.ones((3, keys), bf16),
                jnp.zeros((HEAD_DIM - 4, keys), bf16),
            ]
        )
        heads_low, mixed_t, lse = attend_forward(query_t, pairs, aug)

        def to_tokens(value):
            pieces = value.reshape((groups, rows) + value.shape[1:])
            got = [pieces[0]] + [swap_group(pieces[e], e) for e in range(1, groups)]
            return jnp.stack(got)[group ^ jnp.arange(groups)]

        def to_heads(value):
            value = value[group ^ jnp.arange(groups)]
            got = [value[0]] + [swap_group(value[e], e) for e in range(1, groups)]
            return jnp.concatenate(got, axis=0)

        mixed_low = to_tokens(heads_low).transpose(1, 0, 2).reshape(rows, model)
        branch = dot(mixed_low, out_full, 1, 0) + bias_out.astype(f32)
        normed, scaled_one, inverse_one = norm_forward(source + branch, gain_first, shift_first)
        normed_low = normed.astype(bf16)
        upward = dot(normed_low, up_full, 1, 0) + bias_up.astype(f32)
        active, slope = gelu_both(upward)
        active_low = active.astype(bf16)
        second = dot(active_low, down_full, 1, 0) + bias_down.astype(f32)
        result, scaled_two, inverse_two = norm_forward(normed + second, gain_second, shift_second)

        grad_result = cotangent[0].astype(f32) * row_valid[:, None]
        grad_sum_two, grad_gain_second, grad_shift_second = norm_backward(
            grad_result, gain_second, scaled_two, inverse_two
        )
        grad_second = grad_sum_two.astype(bf16)
        grad_down = dot(active_low, grad_second, 0, 0)
        grad_bias_down = column_sum(grad_second)
        grad_upward = (dot(grad_second, down_full, 1, 1) * slope).astype(bf16)
        grad_up = dot(normed_low, grad_upward, 0, 0)
        grad_bias_up = column_sum(grad_upward)
        grad_normed = grad_sum_two + dot(grad_upward, up_full, 1, 1)
        grad_sum_one, grad_gain_first, grad_shift_first = norm_backward(
            grad_normed, gain_first, scaled_one, inverse_one
        )
        grad_branch = grad_sum_one.astype(bf16)
        grad_out_proj = dot(mixed_low, grad_branch, 0, 0)
        grad_bias_out = column_sum(grad_branch)
        grad_mixed = dot(grad_branch, out_full, 1, 1).astype(bf16)
        grad_heads = to_heads(grad_mixed.reshape(rows, groups, width).transpose(1, 0, 2))

        dq, dk, dv = attend_backward(query_t, pairs, aug, mixed_t, lse, grad_heads)
        dkv = jnp.concatenate([dk, dv], axis=1)
        class_rows = groups * rows
        total = dkv[:class_rows].astype(f32)
        for d in range(1, peers):
            total += swap_peer(dkv[d * class_rows : (d + 1) * class_rows], d).astype(f32)
        dqkv = jnp.concatenate([dq, total.astype(bf16)], axis=1)

        w_joined = w_heads.transpose(1, 0, 2).reshape(model, 3 * width)
        partial = dot(dqkv, w_joined, 1, 1).astype(bf16).reshape(groups, rows, model)
        grad_input = grad_sum_one + partial[0].astype(f32)
        for e in range(1, groups):
            grad_input += swap_group(partial[e], e).astype(f32)

        grad_heads_w = dot(x, dqkv, 0, 0).astype(bf16).reshape(shards, small_rows, 3 * width)
        spread = lax.all_to_all(grad_heads_w, "shard", 0, 0, tiled=True)
        spread = spread.reshape(groups, peers, small_rows, 3, width).astype(f32).sum(axis=1)
        part_heads = spread.transpose(2, 1, 0, 3).reshape(3 * small_rows, model)

        scatter = lambda value: lax.psum_scatter(
            value.astype(bf16), "shard", scatter_dimension=0, tiled=True
        ).astype(f32)
        part_out = scatter(grad_out_proj)
        part_up = scatter(grad_up).reshape(small_rows, -1, model)
        part_down = scatter(grad_down)
        parts = jnp.concatenate(
            [
                part_heads,
                part_out,
                part_up.transpose(1, 0, 2).reshape(-1, model),
                part_down,
            ]
        ).astype(bf16)
        shared = across_reps(parts).reshape((reps, -1, model)).astype(f32).sum(axis=0)
        shared = across_reps(
            jnp.broadcast_to(shared.astype(bf16)[None], (reps,) + shared.shape).reshape(-1, model)
        ).astype(f32)
        sum_query, sum_key, sum_value, sum_out = (
            shared[i * small_rows : (i + 1) * small_rows] for i in range(4)
        )
        up_rows = small_rows * (w_up.shape[1] // model)
        sum_up = shared[4 * small_rows : 4 * small_rows + up_rows]
        sum_up = sum_up.reshape(-1, small_rows, model).transpose(1, 0, 2).reshape(w_up.shape)
        sum_down = shared[4 * small_rows + up_rows :]

        head_bias = jnp.stack([column_sum(dqkv[:, :width]), column_sum(dqkv[:, 2 * width :])])
        placed = jnp.zeros((2, groups, width), f32)
        placed = lax.dynamic_update_slice(placed, head_bias[:, None], (0, group, 0))
        vectors = [placed[0].reshape(-1), placed[1].reshape(-1)] + [
            grad_bias_out,
            grad_gain_first,
            grad_shift_first,
            grad_bias_up,
            grad_bias_down,
            grad_gain_second,
            grad_shift_second,
        ]
        sizes = [v.shape[0] // shards for v in vectors]
        stacked = jnp.concatenate([v.reshape(shards, -1) for v in vectors], axis=1)
        every = jnp.broadcast_to(stacked[None], (reps,) + stacked.shape).reshape(-1, stacked.shape[1])
        every = lax.all_to_all(every, ("rep", "shard"), 0, 0, tiled=True).sum(axis=0)
        sums = []
        start = 0
        for size in sizes:
            sums.append(every[start : start + size])
            start += size
        return (
            result.astype(bf16)[None],
            grad_input[None],
            sum_query,
            sum_key,
            sum_value,
            sum_out,
            sums[0],
            sums[1],
            sums[2],
            sums[3],
            sums[4],
            sum_up,
            sums[5],
            sum_down,
            sums[6],
            sums[7],
            sums[8],
        )

    return body


def solution(mesh):
    rows, vector, token = P("shard", None), P("shard"), P("rep", "shard", None)
    params = (rows,) * 4 + (vector,) * 5 + (rows, vector, rows) + (vector,) * 3
    return jax.shard_map(
        make_body(mesh.shape["rep"], mesh.shape["shard"]),
        mesh=mesh,
        in_specs=(token, token, P("rep")) + params,
        out_specs=(token, token) + params,
        check_vma=False,
    )
```

time: 740 us -> 449 us (0.61)
  waiting for transfers between devices: 421 us -> 223 us
  matrix products: 97.8 us -> 40.6 us
  blocking collectives: 79.9 us -> 40 us
  starting transfers between devices: 0.6 us -> 39.2 us
  local copies, waits for them, and re-layouts: 73.4 us -> 37.5 us
  Pallas kernels: 0 us -> 32 us
  other arithmetic: 46.8 us -> 20.6 us
    unnamed x19 -> x6, waiting for transfers between devices: 135 us -> 1.44 us
    all_gather x7 -> x3, waiting for transfers between devices: 123 us -> 16.3 us  [the longest x1 16.2 us: body(): down_full = lax.all_gather(w_down, 'shard', axis=0, tiled=True)]
    reduce_scatter x3, waiting for transfers between devices: 143 us -> 55.7 us  [body(): lax.psum_scatter(value.astype(bf16), 'shard', scatter_dimension=0, tiled=...]
    all_to_all x0 -> x4, waiting for transfers between devices: none -> 84.3 us  [the longest x1 60.2 us: body(): lax.all_to_all(packed, 'shard', 0, 0, tiled=True, axis_index_groups=zg)]
    ppermute x0 -> x16, waiting for transfers between devices: none -> 64.8 us  [the longest x12 61.5 us: swap_group(): return lax.ppermute(value, 'shard', perm)]
    dot_general x67 -> x14, matrix products: 97.8 us -> 40.6 us  [dot(): lax.dot_general(left, right, (((left_dim,), (right_dim,)), ((), ())), pre...]
    unnamed x2 -> x0, blocking collectives: 56.8 us -> none
    all_to_all x0 -> x1, blocking collectives: none -> 40 us  [body(): spread = lax.all_to_all(grad_heads_w, 'shard', 0, 0, tiled=True)]
  transfers between devices with their start and end apart: 15 -> 26, of which waited for: 13 -> 15; matrix products, arithmetic and copies ran while one was open for 18% -> 15% of each run, Pallas kernels for 0% -> 7%
where the time goes in v1:
time: 449 us; the launch traced here: 448 us
  waiting for transfers between devices  223 us (50%)
  matrix products  40.6 us (9%)
  blocking collectives  40 us (9%)
  starting transfers between devices  39.2 us (9%)
  local copies, waits for them, and re-layouts  37.5 us (8%)
  Pallas kernels  32 us (7%)
  other arithmetic  20.6 us (5%)
  between operations  15.6 us (3%)
    ppermute x12, waiting for transfers between devices, swap_group(): return lax.ppermute(value, 'shard', perm)  61.5 us
    all_to_all x1, waiting for transfers between devices, body(): lax.all_to_all(packed, 'shard', 0, 0, tiled=True, axis_index_groups=zg)  60.2 us
    reduce_scatter x3, waiting for transfers between devices, body(): lax.psum_scatter(value.astype(bf16), 'shard', scatter_dimension=0, tiled=...  55.7 us
    dot_general x14, matrix products, dot(): lax.dot_general(left, right, (((left_dim,), (right_dim,)), ((), ())), pre...  40.6 us
    all_to_all x1, blocking collectives, body(): spread = lax.all_to_all(grad_heads_w, 'shard', 0, 0, tiled=True)  40 us
    ppermute x12, starting transfers between devices, swap_group(): return lax.ppermute(value, 'shard', perm)  20.3 us
    all_to_all x2, waiting for transfers between devices, across_reps(): return lax.all_to_all(value, 'rep', 0, 0, tiled=True)  17.6 us
    pallas_call x1, Pallas kernels, attend_backward(): pl.pallas_call(lambda *refs: backward_kernel(*refs, block=block), out_sha...  17.5 us
  transfers between devices with their start and end apart: 26, of which 15 were waited for; matrix products, arithmetic and copies ran while one was open for 15% of the time, Pallas kernels for 7%

profile of v1, /device:TPU:0, one launch (start us, length us, event | category | flops | bytes accessed | tf_op | source)
XLA Modules:
  0.0 447.9 jit_solution(1452626502991719646)
XLA Ops:
  7.3 4.9 %concatenate.39 = bf16[1536]{0:T(1024)(128)(2,1)S(1)} concatenate(bf16[96]{0:T(256)(128)(2,1)} %param.27, bf16[96]{0:T(256)(128)(2,1)} %param.28, bf16[96]{0:T(256)(128)(2,1)} %param.29, bf16[384]{0:T(512)(128)(2,1)} %param.31, bf16[96]{0:T(256)(128)(2,1)} %param.33, bf16[96]{0:T(256)(128)(2,1)} %param.34, bf16[96]{0:T(256)(128)(2,1)} %param.35, bf16[576]{0:T(1024)(128)(2,1)S(1)} %broadcast_in_dim.30), dimensions={0} | concatenate | bytes 6144 | tf_op jit(solution)/shard_map/concatenate | solution.py:265
  15.3 5.1 %collective-permute-start.3 = (bf16[224,768]{1,0:T(8,128)(2,1)}, bf16[224,768]{1,0:T(8,128)(2,1)}, u32[]{:S(2)}, u32[]{:S(2)}) collective-permute-start(bf16[224,768]{1,0:T(8,128)(2,1)} %bitcast.118), channel_id=1, source_target_pairs={{0,6},{1,7},{2,4},{3,5},{4,2},{5,3},{6,0},{7,1},{8,14},{9,15},{10,... | collective-permute-start | bytes 1032200 | tf_op jit(solution)/shard_map/ppermute | solution.py:203
  23.5 5.0 %all-to-all-start = ((bf16[4,3,96,192]{3,2,1,0:T(8,128)(2,1)}), bf16[4,3,96,192]{3,2,1,0:T(8,128)(2,1)S(1)}, u32[]{:S(2)}, u32[]{:S(2)}) async-start(bf16[4,3,96,192]{3,2,1,0:T(8,128)(2,1)} %maximum_bitcast_fusion), calls=%async_computation | async-start | bytes 1179648 | tf_op jit(solution)/shard_map/all_to_all | solution.py:253
  29.4 60.2 %all-to-all-done = bf16[4,3,96,192]{3,2,1,0:T(8,128)(2,1)S(1)} async-done(((bf16[4,3,96,192]{3,2,1,0:T(8,128)(2,1)}), bf16[4,3,96,192]{3,2,1,0:T(8,128)(2,1)S(1)}, u32[]{:S(2)}, u32[]{:S(2)}) %all-to-all-start) | async-done | bytes 442400 | tf_op jit(solution)/shard_map/all_to_all | solution.py:253
  104.9 14.5 %attend_forward.1 = (bf16[896,192]{1,0:T(8,128)(2,1)}, f32[192,896]{1,0:T(8,128)}, f32[8,896]{1,0:T(8,128)}) custom-call(bf16[192,896]{1,0:T(8,128)(2,1)} %fusion.9.refs_0_, bf16[384,1792]{1,0:T(8,128)(2,1)} %pad_maximum_fusion.2.refs_1_, bf16[64,1792]{1,0:T(8,128)(2,1)} %maximum_maximum_fusion.refs_2_), custom_call_target="tpu_custom_call" | custom-call | tf_op jit(solution)/shard_map/attend_forward/pallas_call | solution.py:138
  120.5 5.9 %collective-permute-start.8 = (bf16[224,192]{1,0:T(8,128)(2,1)S(1)}, bf16[224,192]{1,0:T(8,128)(2,1)S(1)}, u32[]{:S(2)}, u32[]{:S(2)}) collective-permute-start(bf16[224,192]{1,0:T(8,128)(2,1)S(1)} %get-tuple-element.57), channel_id=1, source_target_pairs={{0,6},{1,7},{2,4},{3,5},{4,2},{5,3},{6,0},{7,1},{8,14},{9,15},{10,... | collective-permute-start | bytes 258056 | tf_op jit(solution)/shard_map/ppermute | solution.py:203
  127.1 5.8 %collective-permute-done.8 = bf16[224,192]{1,0:T(8,128)(2,1)S(1)} collective-permute-done((bf16[224,192]{1,0:T(8,128)(2,1)S(1)}, bf16[224,192]{1,0:T(8,128)(2,1)S(1)}, u32[]{:S(2)}, u32[]{:S(2)}) %collective-permute-start.8) | collective-permute-done | bytes 86048 | tf_op jit(solution)/shard_map/ppermute | solution.py:203
  132.9 14.1 %collective-permute-done.7 = bf16[224,192]{1,0:T(8,128)(2,1)S(1)} collective-permute-done((bf16[224,192]{1,0:T(8,128)(2,1)S(1)}, bf16[224,192]{1,0:T(8,128)(2,1)S(1)}, u32[]{:S(2)}, u32[]{:S(2)}) %collective-permute-start.7) | collective-permute-done | bytes 86048 | tf_op jit(solution)/shard_map/ppermute | solution.py:203
  152.7 6.0 %multiply_convert_fusion = (bf16[224,3072]{1,0:T(8,128)(2,1)}, f32[224,3072]{1,0:T(8,128)}) fusion(f32[3072]{0:T(1024)S(1)} %reshape.404, bf16[768,3072]{1,0:T(8,128)(2,1)} %all-gather.6.cloned.1.call-done, f32[224,768]{1,0:T(8,128)S(1)} %get-tuple-element.81, f32[768]{0:T(1024)S(1)} %reshape.403, f32[768]{0:T(1024)S(1)} %reshape.402, ...), kind=kOutput, calls=%fused_computation.15 | convolution fusion | flops 1061953536 | bytes 9555712 | tf_op jit(solution)/shard_map/dot_general | solution.py:21
  158.7 16.2 %all-gather.8.cloned.1.call-done = bf16[3072,768]{1,0:T(8,128)(2,1)} async-done(((bf16[384,768]{1,0:T(8,128)(2,1)}), bf16[3072,768]{1,0:T(8,128)(2,1)}) %all-gather.8.cloned.1.call-update) | async-done | bytes 4718608 | tf_op jit(solution)/shard_map/all_gather | solution.py:291
  174.9 4.2 fusion.44
  189.1 4.6 %multiply_reduce_fusion = (f32[768]{0:T(1024)S(1)}, f32[224]{0:T(256)S(1)}, f32[224]{0:T(256)S(1)}, f32[768]{0:T(1024)S(1)}, f32[224,768]{1,0:T(8,128)S(1)}) fusion(f32[224,768]{1,0:T(8,128)S(1)} %get-tuple-element.81, f32[224]{0:T(256)S(1)} %add_rsqrt_fusion.1, f32[224]{0:T(256)S(1)} %broadcast_multiply_fusion.5, f32[768]{0:T(1024)S(1)} %reshape.402, ...), kind=kOutput, calls=%fused_computation.59 | convolution fusion | flops 1058682880 | bytes 8172032 | tf_op jit(solution)/shard_map/dot_general | solution.py:21
  195.6 5.0 %convolution_convert_fusion = bf16[3072,768]{1,0:T(8,128)(2,1)} fusion(bf16[224,3072]{1,0:T(8,128)(2,1)} %get-tuple-element.82, f32[224,768]{1,0:T(8,128)S(1)} %copy-done.6), kind=kOutput, calls=%fused_computation.4 | convolution fusion | flops 1059495936 | bytes 6782976 | tf_op jit(solution)/shard_map/dot_general | solution.py:21
  208.0 5.8 %collective-permute-done.11 = bf16[224,192]{1,0:T(8,128)(2,1)S(1)} collective-permute-done((bf16[224,192]{1,0:T(8,128)(2,1)S(1)}, bf16[224,192]{1,0:T(8,128)(2,1)S(1)}, u32[]{:S(2)}, u32[]{:S(2)}) %collective-permute-start.11) | collective-permute-done | bytes 86048 | tf_op jit(solution)/shard_map/ppermute | solution.py:203
  213.8 5.8 %collective-permute-done.9 = bf16[224,192]{1,0:T(8,128)(2,1)S(1)} collective-permute-done((bf16[224,192]{1,0:T(8,128)(2,1)S(1)}, bf16[224,192]{1,0:T(8,128)(2,1)S(1)}, u32[]{:S(2)}, u32[]{:S(2)}) %collective-permute-start.9) | collective-permute-done | bytes 86048 | tf_op jit(solution)/shard_map/ppermute | solution.py:203
  221.4 17.5 %attend_backward.1 = (bf16[896,192]{1,0:T(8,128)(2,1)}, bf16[1792,192]{1,0:T(8,128)(2,1)}, bf16[1792,192]{1,0:T(8,128)(2,1)}) custom-call(bf16[192,896]{1,0:T(8,128)(2,1)} %fusion.9.refs_0_, bf16[384,1792]{1,0:T(8,128)(2,1)} %pad_maximum_fusion.2.refs_1_, bf16[64,1792]{1,0:T(8,128)(2,1)} %maximum_maximum_fusion.refs_2_, ...), custom_call_target="tpu_custom_call" | custom-call | tf_op jit(solution)/shard_map/attend_backward/pallas_call | solution.py:158
  249.0 40.0 %all_to_all.31 = bf16[8,96,576]{2,1,0:T(8,128)(2,1)S(1)} all-to-all(bf16[8,96,576]{2,1,0:T(8,128)(2,1)S(1)} %bitcast.105), channel_id=1, replica_groups=mesh['rep'=4,'shard'=8] {'shard'}, dimensions={0} | all-to-all | bytes 1769472 | tf_op jit(solution)/shard_map/all_to_all | solution.py:367
  292.6 55.6 %reduce-scatter.8.cloned.1.call-done = bf16[384,768]{1,0:T(8,128)(2,1)} async-done(((bf16[3072,768]{1,0:T(8,128)(2,1)}), bf16[384,768]{1,0:T(8,128)(2,1)}) %reduce-scatter.8.cloned.1.call-update) | async-done | bytes 589840 | tf_op jit(solution)/shard_map/reduce_scatter | solution.py:371
  350.7 4.8 %all-to-all-start.2 = ((bf16[4,288,768]{2,1,0:T(8,128)(2,1)}), bf16[4,288,768]{2,1,0:T(8,128)(2,1)}, u32[]{:S(2)}, u32[]{:S(2)}) async-start(bf16[4,288,768]{2,1,0:T(8,128)(2,1)} %bitcast.103), calls=%async_computation.5 | async-start | bytes 3538944 | tf_op jit(solution)/shard_map/all_to_all | solution.py:210
  357.5 17.6 %all-to-all-done.2 = bf16[4,288,768]{2,1,0:T(8,128)(2,1)} async-done(((bf16[4,288,768]{2,1,0:T(8,128)(2,1)}), bf16[4,288,768]{2,1,0:T(8,128)(2,1)}, u32[]{:S(2)}, u32[]{:S(2)}) %all-to-all-start.2) | async-done | bytes 1769504 | tf_op jit(solution)/shard_map/all_to_all | solution.py:210
  381.0 6.4 %all-to-all-done.4 = f32[32,1,1152]{2,1,0:T(1,128)S(1)} async-done(((f32[32,1,1152]{2,1,0:T(1,128)}), f32[32,1,1152]{2,1,0:T(1,128)S(1)}, u32[]{:S(2)}, u32[]{:S(2)}) %all-to-all-start.4) | async-done | bytes 147488 | tf_op jit(solution)/shard_map/all_to_all | solution.py:412
  388.8 4.4 all-to-all-start.3
  404.9 12.4 %collective-permute-done.13 = bf16[224,768]{1,0:T(8,128)(2,1)S(1)} collective-permute-done((bf16[224,768]{1,0:T(8,128)(2,1)}, bf16[224,768]{1,0:T(8,128)(2,1)S(1)}, u32[]{:S(2)}, u32[]{:S(2)}) %collective-permute-start.13) | collective-permute-done | bytes 344096 | tf_op jit(solution)/shard_map/ppermute | solution.py:203
  418.6 15.4 %collective-permute-done.14 = bf16[224,768]{1,0:T(8,128)(2,1)} collective-permute-done((bf16[224,768]{1,0:T(8,128)(2,1)S(1)}, bf16[224,768]{1,0:T(8,128)(2,1)}, u32[]{:S(2)}, u32[]{:S(2)}) %collective-permute-start.14) | collective-permute-done | bytes 344096 | tf_op jit(solution)/shard_map/ppermute | solution.py:203
  (226 shorter events, 94.9 us)
Async XLA Ops:
  7.2 140.7 %all-gather.10.cloned.1.call-start = ((), (), s32[]{:S(2)}) async-start(), calls=%async_computation.13 | async-start | bytes 1437696 | tf_op jit(solution)/shard_map/all_gather | solution.py:261
  13.8 138.8 %all-gather.6.cloned.1.call-start = ((), (), s32[]{:S(2)}) async-start(), calls=%async_computation.8 | async-start | bytes 5308416 | tf_op jit(solution)/shard_map/all_gather | solution.py:290
  14.6 160.4 %all-gather.8.cloned.1.call-start = ((), (), s32[]{:S(2)}) async-start(), calls=%async_computation.9 | async-start | bytes 5308416 | tf_op jit(solution)/shard_map/all_gather | solution.py:291
  15.3 79.3 %collective-permute-start.3 = (bf16[224,768]{1,0:T(8,128)(2,1)}, bf16[224,768]{1,0:T(8,128)(2,1)}, u32[]{:S(2)}, u32[]{:S(2)}) collective-permute-start(bf16[224,768]{1,0:T(8,128)(2,1)} %bitcast.118), channel_id=1, source_target_pairs={{0,6},{1,7},{2,4},{3,5},{4,2},{5,3},{6,0},{7,1},{8,14},{9,15},{10,... | collective-permute-start | bytes 1032200 | tf_op jit(solution)/shard_map/ppermute | solution.py:203
  20.4 74.2 %collective-permute-start.2 = (bf16[224,768]{1,0:T(8,128)(2,1)}, bf16[224,768]{1,0:T(8,128)(2,1)}, u32[]{:S(2)}, u32[]{:S(2)}) collective-permute-start(bf16[224,768]{1,0:T(8,128)(2,1)} %bitcast.119), channel_id=1, source_target_pairs={{0,4},{1,5},{2,6},{3,7},{4,0},{5,1},{6,2},{7,3},{8,12},{9,13},{10,... | collective-permute-start | bytes 1032200 | tf_op jit(solution)/shard_map/ppermute | solution.py:203
  20.4 74.2 %collective-permute-start.1 = (bf16[224,768]{1,0:T(8,128)(2,1)}, bf16[224,768]{1,0:T(8,128)(2,1)}, u32[]{:S(2)}, u32[]{:S(2)}) collective-permute-start(bf16[224,768]{1,0:T(8,128)(2,1)} %bitcast.120), channel_id=1, source_target_pairs={{0,2},{1,3},{2,0},{3,1},{4,6},{5,7},{6,4},{7,5},{8,10},{9,11},{10,... | collective-permute-start | bytes 1032200 | tf_op jit(solution)/shard_map/ppermute | solution.py:203
  21.8 68.2 %collective-permute-start.4 = (bf16[2,96]{1,0:T(2,128)(2,1)S(1)}, bf16[2,96]{1,0:T(2,128)(2,1)S(1)}, u32[]{:S(2)}, u32[]{:S(2)}) collective-permute-start(bf16[2,96]{1,0:T(2,128)(2,1)S(1)} %pad_maximum_fusion.13), channel_id=1, source_target_pairs={{0,1},{1,0},{2,3},{3,2},{4,5},{5,4},{6,7},{7,6},{8,9},{9,8},{10,11... | collective-permute-start | bytes 1160 | tf_op jit(solution)/shard_map/ppermute | solution.py:207
  23.5 66.1 %all-to-all-start = ((bf16[4,3,96,192]{3,2,1,0:T(8,128)(2,1)}), bf16[4,3,96,192]{3,2,1,0:T(8,128)(2,1)S(1)}, u32[]{:S(2)}, u32[]{:S(2)}) async-start(bf16[4,3,96,192]{3,2,1,0:T(8,128)(2,1)} %maximum_bitcast_fusion), calls=%async_computation | async-start | bytes 1179648 | tf_op jit(solution)/shard_map/all_to_all | solution.py:253
  28.5 262.2 %reduce-scatter.6.cloned.1.call-start = ((), (), s32[]{:S(2)}) async-start(), calls=%async_computation.11 | async-start | bytes 5308416 | tf_op jit(solution)/shard_map/reduce_scatter | solution.py:371
  99.2 4.4 collective-permute-start.5
  120.5 12.4 %collective-permute-start.8 = (bf16[224,192]{1,0:T(8,128)(2,1)S(1)}, bf16[224,192]{1,0:T(8,128)(2,1)S(1)}, u32[]{:S(2)}, u32[]{:S(2)}) collective-permute-start(bf16[224,192]{1,0:T(8,128)(2,1)S(1)} %get-tuple-element.57), channel_id=1, source_target_pairs={{0,6},{1,7},{2,4},{3,5},{4,2},{5,3},{6,0},{7,1},{8,14},{9,15},{10,... | collective-permute-start | bytes 258056 | tf_op jit(solution)/shard_map/ppermute | solution.py:203
  126.4 20.5 %collective-permute-start.7 = (bf16[224,192]{1,0:T(8,128)(2,1)S(1)}, bf16[224,192]{1,0:T(8,128)(2,1)S(1)}, u32[]{:S(2)}, u32[]{:S(2)}) collective-permute-start(bf16[224,192]{1,0:T(8,128)(2,1)S(1)} %get-tuple-element.58), channel_id=1, source_target_pairs={{0,4},{1,5},{2,6},{3,7},{4,0},{5,1},{6,2},{7,3},{8,12},{9,13},{10,... | collective-permute-start | bytes 258056 | tf_op jit(solution)/shard_map/ppermute | solution.py:203
  126.4 20.5 %collective-permute-start.6 = (bf16[224,192]{1,0:T(8,128)(2,1)S(1)}, bf16[224,192]{1,0:T(8,128)(2,1)S(1)}, u32[]{:S(2)}, u32[]{:S(2)}) collective-permute-start(bf16[224,192]{1,0:T(8,128)(2,1)S(1)} %get-tuple-element.59), channel_id=1, source_target_pairs={{0,2},{1,3},{2,0},{3,1},{4,6},{5,7},{6,4},{7,5},{8,10},{9,11},{10,... | collective-permute-start | bytes 258056 | tf_op jit(solution)/shard_map/ppermute | solution.py:203
  188.0 104.6 %reduce-scatter.4.cloned.1.call-start = ((), (), s32[]{:S(2)}) async-start(), calls=%async_computation.10 | async-start | bytes 1327104 | tf_op jit(solution)/shard_map/reduce_scatter | solution.py:371
  195.5 152.7 %reduce-scatter.8.cloned.1.call-start = ((), (), s32[]{:S(2)}) async-start(), calls=%async_computation.12 | async-start | bytes 5308416 | tf_op jit(solution)/shard_map/reduce_scatter | solution.py:371
  203.5 10.3 %collective-permute-start.11 = (bf16[224,192]{1,0:T(8,128)(2,1)S(1)}, bf16[224,192]{1,0:T(8,128)(2,1)S(1)}, u32[]{:S(2)}, u32[]{:S(2)}) collective-permute-start(bf16[224,192]{1,0:T(8,128)(2,1)S(1)} %bitcast.130), channel_id=1, source_target_pairs={{0,6},{1,7},{2,4},{3,5},{4,2},{5,3},{6,0},{7,1},{8,14},{9,15},{10,... | collective-permute-start | bytes 258056 | tf_op jit(solution)/shard_map/ppermute | solution.py:203
  204.9 14.7 %collective-permute-start.9 = (bf16[224,192]{1,0:T(8,128)(2,1)S(1)}, bf16[224,192]{1,0:T(8,128)(2,1)S(1)}, u32[]{:S(2)}, u32[]{:S(2)}) collective-permute-start(bf16[224,192]{1,0:T(8,128)(2,1)S(1)} %bitcast.129), channel_id=1, source_target_pairs={{0,2},{1,3},{2,0},{3,1},{4,6},{5,7},{6,4},{7,5},{8,10},{9,11},{10,... | collective-permute-start | bytes 258056 | tf_op jit(solution)/shard_map/ppermute | solution.py:203
  204.9 15.6 %collective-permute-start.10 = (bf16[224,192]{1,0:T(8,128)(2,1)S(1)}, bf16[224,192]{1,0:T(8,128)(2,1)S(1)}, u32[]{:S(2)}, u32[]{:S(2)}) collective-permute-start(bf16[224,192]{1,0:T(8,128)(2,1)S(1)} %bitcast.128), channel_id=1, source_target_pairs={{0,4},{1,5},{2,6},{3,7},{4,0},{5,1},{6,2},{7,3},{8,12},{9,13},{10,... | collective-permute-start | bytes 258056 | tf_op jit(solution)/shard_map/ppermute | solution.py:203
  350.7 24.4 %all-to-all-start.2 = ((bf16[4,288,768]{2,1,0:T(8,128)(2,1)}), bf16[4,288,768]{2,1,0:T(8,128)(2,1)}, u32[]{:S(2)}, u32[]{:S(2)}) async-start(bf16[4,288,768]{2,1,0:T(8,128)(2,1)} %bitcast.103), calls=%async_computation.5 | async-start | bytes 3538944 | tf_op jit(solution)/shard_map/all_to_all | solution.py:210
  375.1 12.4 %all-to-all-start.4 = ((f32[32,1,1152]{2,1,0:T(1,128)}), f32[32,1,1152]{2,1,0:T(1,128)S(1)}, u32[]{:S(2)}, u32[]{:S(2)}) async-start(f32[32,1,1152]{2,1,0:T(1,128)} %all_to_all.24), calls=%async_computation.7 | async-start | bytes 294912 | tf_op jit(solution)/shard_map/all_to_all | solution.py:412
  388.8 47.3 %all-to-all-start.3 = ((bf16[4,288,768]{2,1,0:T(8,128)(2,1)}), bf16[4,288,768]{2,1,0:T(8,128)(2,1)}, u32[]{:S(2)}, u32[]{:S(2)}) async-start(bf16[4,288,768]{2,1,0:T(8,128)(2,1)} %broadcast_in_dim.33), calls=%async_computation.6 | async-start | bytes 3538944 | tf_op jit(solution)/shard_map/all_to_all | solution.py:210
  400.1 17.3 %collective-permute-start.13 = (bf16[224,768]{1,0:T(8,128)(2,1)}, bf16[224,768]{1,0:T(8,128)(2,1)S(1)}, u32[]{:S(2)}, u32[]{:S(2)}) collective-permute-start(bf16[224,768]{1,0:T(8,128)(2,1)} %get-tuple-element.49), channel_id=1, source_target_pairs={{0,2},{1,3},{2,0},{3,1},{4,6},{5,7},{6,4},{7,5},{8,10},{9,11},{10,... | collective-permute-start | bytes 1032200 | tf_op jit(solution)/shard_map/ppermute | solution.py:203
  400.6 18.0 %collective-permute-start.15 = (bf16[224,768]{1,0:T(8,128)(2,1)}, bf16[224,768]{1,0:T(8,128)(2,1)S(1)}, u32[]{:S(2)}, u32[]{:S(2)}) collective-permute-start(bf16[224,768]{1,0:T(8,128)(2,1)} %get-tuple-element.50), channel_id=1, source_target_pairs={{0,6},{1,7},{2,4},{3,5},{4,2},{5,3},{6,0},{7,1},{8,14},{9,15},{10,... | collective-permute-start | bytes 1032200 | tf_op jit(solution)/shard_map/ppermute | solution.py:203
  402.0 32.0 %collective-permute-start.14 = (bf16[224,768]{1,0:T(8,128)(2,1)S(1)}, bf16[224,768]{1,0:T(8,128)(2,1)}, u32[]{:S(2)}, u32[]{:S(2)}) collective-permute-start(bf16[224,768]{1,0:T(8,128)(2,1)S(1)} %get-tuple-element.51), channel_id=1, source_target_pairs={{0,4},{1,5},{2,6},{3,7},{4,0},{5,1},{6,2},{7,3},{8,12},{9,13},{10,... | collective-permute-start | bytes 1032200 | tf_op jit(solution)/shard_map/ppermute | solution.py:203
  (28 other events, 125.2 us)
Sparse Core Ops, SparseCore 0:
  13.9 39.2 all-gather.9
  54.9 57.5 all-gather.5
  114.2 60.7 all-gather.7
  188.1 59.8 reduce-scatter.5
  250.8 38.4 reduce-scatter.3
  291.4 56.7 reduce-scatter.7
